TPU v7x, 512 devices: a whole 4x8x8 slice. The times are simulated.
512 devices in a mesh: prompt: 16 (over x, y_lo), feat: 32 (over y_hi, z, core).
Axes of the slice: x: 4, y: 8 (y_hi: 2, y_lo: 4; y = y_hi * 4 + y_lo), z: 8, core: 2. Of those that a mesh axis runs over, the one named last changes fastest.
Arguments:
- decoder: bfloat16 [8192, 5376], P('feat'), may hold values from -0.078125 to 0.078125
- encoder: bfloat16 [24576, 5376], P(('feat', 'prompt')), may hold values from -6 to 6
- row_ids: int32 [16, 512], P('prompt', 'feat'), may hold values from 0 to 255
- counts: int32 [16, 32], P('prompt'), may hold values from 1 to 16, 307 in all within a row
- activity: float32 [16, 512], P('prompt'), may hold values from 0.25 to 4
Outputs:
- edges: bfloat16 [16, 512, 24576], P('prompt', None, 'feat')
Inputs may be any that keep to these rules, and one draw needn't show every extreme that they name: counts of one prompt sum to 307; some owner of each prompt holds exactly 16.
All inputs are finite; a program needn't handle non-finite values.
Results may differ from a plain program's by a relative error of at most 0.001.
Values may be sent and summed in bfloat16 or wider, within the bound.
No kernel may reach another device: no remote copies, remote signals or barrier semaphores. Data moves between devices by JAX's collectives and lax.ppermute only.
A program may use at most 64 MiB of HBM per device.

v0:
```python
import jax
import jax.numpy as jnp
from jax import lax
from jax.sharding import PartitionSpec as P


def per_device(decoder, encoder, row_ids, counts, activity):
    slot_count = row_ids.shape[1]
    owner_index = lax.axis_index("feat")
    picked_rows = jnp.take(decoder, row_ids[0], axis=0)
    live_count = lax.dynamic_index_in_dim(counts[0], owner_index, 0, keepdims=False)
    live_slots = jnp.arange(slot_count, dtype=jnp.int32) < live_count
    source_rows = jnp.where(live_slots[:, None], picked_rows, jnp.zeros((), picked_rows.dtype))
    weights = activity[0]
    whole_rows = lax.all_gather(source_rows, "feat", axis=0, tiled=True)
    products = lax.dot_general(
        whole_rows,
        lax.all_gather(encoder, "prompt", axis=0, tiled=True),
        (((1,), (1,)), ((), ())),
        preferred_element_type=jnp.float32,
    )
    edges = (weights[:, None] * products).astype(jnp.bfloat16)
    return edges[None]


def solution(mesh):
    in_specs = (
        P("feat", None),
        P(("feat", "prompt"), None),
        P("prompt", "feat"),
        P("prompt", None),
        P("prompt", None),
    )
    out_specs = P("prompt", None, "feat")
    return jax.shard_map(
        per_device, mesh=mesh, in_specs=in_specs, out_specs=out_specs, check_vma=False
    )
```

profile of v0, /device:TPU:1, one launch (start us, length us, event | category | flops | bytes accessed | tf_op | source)
XLA Modules:
  0.0 330.1 jit_solution(3956088950940566915)
XLA Ops:
  6.5 0.0 copy-start
  6.5 0.0 all-gather.3.cloned.1.call-start
  6.5 0.8 fusion.1
  7.3 1.3 constant_dynamic-slice_fusion
  8.6 1.3 compare_and_fusion
  9.9 0.0 copy-done
  9.9 0.7 gather_fusion
  10.6 0.8 select_select_fusion
  11.4 0.0 all-gather.3.cloned.1.call-update
  11.4 0.0 all-gather.5.cloned.1.call-start
  11.4 0.7 all-gather.5.cloned.1.call-update
  12.1 120.5 %all-gather.3.cloned.1.call-done = bf16[512,5376]{1,0:T(8,128)(2,1)} async-done(((bf16[16,5376]{1,0:T(8,128)(2,1)}), bf16[512,5376]{1,0:T(8,128)(2,1)}) %all-gather.3.cloned.1.call-update) | async-done | bytes 5505040 | tf_op jit(solution)/shard_map/all_gather | solution.py:15
  132.7 180.4 %all-gather.5.cloned.1.call-done = bf16[768,5376]{1,0:T(8,128)(2,1)} async-done(((bf16[48,5376]{1,0:T(8,128)(2,1)}), bf16[768,5376]{1,0:T(8,128)(2,1)}) %all-gather.5.cloned.1.call-update) | async-done | bytes 8257552 | tf_op jit(solution)/shard_map/all_gather | solution.py:18
  313.0 10.2 %fusion = bf16[1,512,768]{2,1,0:T(8,128)(2,1)} fusion(bf16[512,5376]{1,0:T(8,128)(2,1)} %all-gather.3.cloned.1.call-done, bf16[768,5376]{1,0:T(8,128)(2,1)} %all-gather.5.cloned.1.call-done, f32[512]{0:T(512)} %bitcast.12), kind=kOutput, calls=%fused_computation.2 | convolution fusion | flops 4228644864 | bytes 14551040 | tf_op jit(solution)/shard_map/dot_general | solution.py:16
  (1 shorter events, 0.0 us)
Async XLA Ops:
  6.5 3.4 %copy-start = (bf16[256,5376]{1,0:T(8,128)(2,1)S(1)}, bf16[256,5376]{1,0:T(8,128)(2,1)}, u32[]{:S(2)}) copy-start(bf16[256,5376]{1,0:T(8,128)(2,1)} %param.5) | copy-start | bytes 8257540
  6.5 126.1 %all-gather.3.cloned.1.call-start = ((), (), s32[]{:S(2)}) async-start(), calls=%async_computation | async-start | bytes 5677056 | tf_op jit(solution)/shard_map/all_gather | solution.py:15
  11.4 301.6 %all-gather.5.cloned.1.call-start = ((), (), s32[]{:S(2)}) async-start(), calls=%async_computation.1 | async-start | bytes 8773632 | tf_op jit(solution)/shard_map/all_gather | solution.py:18
Sparse Core Ops, SparseCore 0:
  11.5 121.0 all-gather.2
  134.7 178.2 all-gather.4
where the time goes:
time: 330 us
  waiting for transfers between devices  302 us (92%)
  between operations  13.4 us (4%)
  matrix products  10.2 us (3%)
    all_gather x1, waiting for transfers between devices, per_device(): lax.all_gather(encoder, 'prompt', axis=0, tiled=True)  180 us
    all_gather x1, waiting for transfers between devices, per_device(): whole_rows = lax.all_gather(source_rows, 'feat', axis=0, tiled=True)  121 us
    dot_general x1, matrix products, per_device(): lax.dot_general(whole_rows, lax.all_gather(encoder, 'prompt', axis=0, til...  10.2 us
  transfers between devices with their start and end apart: 2, of which 2 were waited for; matrix products, arithmetic and copies ran while one was open for 0% of the time, Pallas kernels for 0%

commit v1 on v0

--- a/solution.py
+++ b/solution.py
@@ -12,7 +12,8 @@
     live_slots = jnp.arange(slot_count, dtype=jnp.int32) < live_count
     source_rows = jnp.where(live_slots[:, None], picked_rows, jnp.zeros((), picked_rows.dtype))
     weights = activity[0]
-    whole_rows = lax.all_gather(source_rows, "feat", axis=0, tiled=True)
+    sent = jnp.stack([source_rows] * lax.axis_size("feat"))
+    whole_rows = jnp.concatenate(lax.all_to_all(sent, "feat", 0, 0), axis=0)
     products = lax.dot_general(
         whole_rows,
         lax.all_gather(encoder, "prompt", axis=0, tiled=True),

time: 330 us -> 334 us (1.012)
  blocking collectives: 0 us -> 174 us
  waiting for transfers between devices: 302 us -> 132 us
    all_to_all x0 -> x1, blocking collectives: none -> 174 us  [per_device(): whole_rows = jnp.concatenate(lax.all_to_all(sent, 'feat', 0, 0), axis=0)]
    all_gather x1 -> x0, waiting for transfers between devices: 121 us -> none  [per_device(): whole_rows = lax.all_gather(source_rows, 'feat', axis=0, tiled=True)]
    all_gather x1, waiting for transfers between devices: 180 us -> 131 us  [per_device(): lax.all_gather(encoder, 'prompt', axis=0, tiled=True)]
  transfers between devices with their start and end apart: 2 -> 1, of which waited for: 2 -> 1; matrix products, arithmetic and copies ran while one was open for 0% -> 1% of each run, Pallas kernels for 0% -> 0%
where the time goes in v1:
time: 334 us
  blocking collectives  174 us (52%)
  waiting for transfers between devices  132 us (40%)
  between operations  13.4 us (4%)
  matrix products  10.3 us (3%)
    all_to_all x1, blocking collectives, per_device(): whole_rows = jnp.concatenate(lax.all_to_all(sent, 'feat', 0, 0), axis=0)  174 us
    all_gather x1, waiting for transfers between devices, per_device(): lax.all_gather(encoder, 'prompt', axis=0, tiled=True)  131 us
    dot_general x1, matrix products, per_device(): lax.dot_general(whole_rows, lax.all_gather(encoder, 'prompt', axis=0, til...  10.3 us
  transfers between devices with their start and end apart: 1, of which 1 were waited for; matrix products, arithmetic and copies ran while one was open for 1% of the time, Pallas kernels for 0%

profile of v1, /device:TPU:1, one launch (start us, length us, event | category | flops | bytes accessed | tf_op | source)
XLA Modules:
  0.0 334.1 jit_solution(10667212578584669589)
XLA Ops:
  6.5 0.0 copy-start
  6.5 0.0 all-gather.2.cloned.1.call-start
  6.5 0.7 all-gather.2.cloned.1.call-update
  7.3 1.3 constant_dynamic-slice_fusion
  8.6 0.7 fusion.1
  9.3 0.0 copy-done
  9.3 0.7 gather_fusion
  9.9 1.3 compare_and_fusion
  11.2 0.1 select_select_fusion
  11.3 0.4 stack.2
  11.7 0.0 copy-start.1
  11.7 173.9 %all_to_all.5 = bf16[32,16,5376]{2,1,0:T(8,128)(2,1)} all-to-all(bf16[32,16,5376]{2,1,0:T(8,128)(2,1)S(1)} %stack.2), channel_id=1, replica_groups=mesh['prompt'=16,'feat'=32] {'feat'}, dimensions={0} | all-to-all | bytes 11010048 | tf_op jit(solution)/shard_map/all_to_all | solution.py:16
  185.7 131.2 %all-gather.2.cloned.1.call-done = bf16[768,5376]{1,0:T(8,128)(2,1)} async-done(((bf16[48,5376]{1,0:T(8,128)(2,1)}), bf16[768,5376]{1,0:T(8,128)(2,1)}) %all-gather.2.cloned.1.call-update) | async-done | bytes 8257552 | tf_op jit(solution)/shard_map/all_gather | solution.py:19
  316.9 0.0 copy-done.1
  316.9 10.3 %fusion = bf16[1,512,768]{2,1,0:T(8,128)(2,1)} fusion(bf16[512,5376]{1,0:T(8,128)(2,1)} %bitcast.13, bf16[768,5376]{1,0:T(8,128)(2,1)} %all-gather.2.cloned.1.call-done, f32[512]{0:T(512)S(1)} %bitcast.14), kind=kOutput, calls=%fused_computation.2 | convolution fusion | flops 4228644864 | bytes 14551040 | tf_op jit(solution)/shard_map/dot_general | solution.py:17
  (1 shorter events, 0.0 us)
Async XLA Ops:
  6.5 2.7 copy-start
  6.5 310.4 %all-gather.2.cloned.1.call-start = ((), (), s32[]{:S(2)}) async-start(), calls=%async_computation.1 | async-start | bytes 8773632 | tf_op jit(solution)/shard_map/all_gather | solution.py:19
  11.7 305.2 %copy-start.1 = (f32[1,512]{1,0:T(1,128)S(1)}, f32[1,512]{1,0:T(1,128)}, u32[]{:S(2)}) copy-start(f32[1,512]{1,0:T(1,128)} %param.9) | copy-start | bytes 6148
Sparse Core Ops, SparseCore 0:
  9.4 307.4 all-gather.1
